TPU v7x, 256 devices: a whole 4x4x8 slice. The times are simulated.
256 devices in a mesh: row: 32 (over y_lo, z, core), col: 8 (over y_hi, x).
Axes of the slice: x: 4, y: 4 (y_hi: 2, y_lo: 2; y = y_hi * 2 + y_lo), z: 8, core: 2. Of those that a mesh axis runs over, the one named last changes fastest.
Arguments:
- left_slots: float32 [32, 4096, 512], P('row', 'col'), may hold values from -0.109375 to 0.109375
- right: float32 [8192, 8192], P('col', 'row'), may hold values from -6 to 6
- previous: float32 [4096, 8192], P('col', 'row'), may hold values from -4 to 4
- offsets: int32 [6], replicated, may hold values from 0 to 15, as said below
- owners: int32 [8, 6], P('col'), may hold values from 0 to 31, as said below
Outputs:
- next_density: float32 [4096, 8192], P('col', 'row')
Inputs may be any that keep to these rules, and one draw needn't show every extreme that they name: `offsets`: distinct, in any order; they include 0 and 15. `owners`: distinct within each grid row.
All inputs are finite; a program needn't handle non-finite values.
Results may differ from a plain program's by a relative error of at most 0.0001.
Values sent between devices are 32-bit elements; how exact they have to be, the bound alone decides.
A program may use at most 64 MiB of HBM per device.

v0:
```python
import jax
import jax.numpy as jnp
from jax import lax
from jax.sharding import PartitionSpec as P


def spread(array, axis, root):
    mine = lax.axis_index(axis) == root
    return lax.psum(jnp.where(mine, array, jnp.zeros_like(array)), axis)


def from_behind(array, axis, by):
    peers = lax.axis_size(axis)
    return lax.ppermute(array, axis, [(i, (i + by) % peers) for i in range(peers)])


def multiply(left_block, right_block):
    return jnp.dot(
        left_block, right_block, precision=lax.Precision.HIGHEST, preferred_element_type=jnp.float32
    )


def shards(left_slots, right, previous, offsets, owners):
    own_block = left_slots[0]
    width = own_block.shape[1]
    count = offsets.shape[0]
    blocks = right.shape[0] // width
    left_list = []
    for number in range(count):
        left_list.append(spread(own_block, "row", owners[0, number]))
    accum_start = jnp.zeros((own_block.shape[0], right.shape[1]), jnp.float32)
    stacked = jnp.stack(left_list)
    numbers = jnp.arange(count, dtype=jnp.int32)

    def add_step(step, moving, accum):
        for slot in range(blocks):
            offset_value = step * blocks + slot
            matched = offsets == offset_value
            present = jnp.any(matched)
            which = jnp.sum(jnp.where(matched, numbers, 0))
            chosen = lax.dynamic_index_in_dim(stacked, which, 0, keepdims=False)
            piece = moving[slot * width : (slot + 1) * width]

            def with_block(current):
                return current + multiply(chosen, piece)

            def without_block(current):
                return current

            accum = lax.cond(present, with_block, without_block, accum)
        return accum

    accum = add_step(0, right, accum_start)

    def turn(step, state):
        moving, current = state
        moving = from_behind(moving, "col", -1)
        return (moving, add_step(step, moving, current))

    moving, accum = lax.fori_loop(1, lax.axis_size("col"), turn, (right, accum))
    return 2.0 * previous - accum


def solution(mesh):
    return jax.shard_map(
        shards,
        mesh=mesh,
        in_specs=(P("row", "col", None), P("col", "row"), P("col", "row"), P(), P("col", None)),
        out_specs=P("col", "row"),
        check_vma=False,
    )
```

profile of v0, /device:TPU:6, one launch (start us, length us, event | category | flops | bytes accessed | tf_op | source)
XLA Modules:
  0.0 492.5 jit_solution(2943840070337642655)
XLA Ops:
  13.1 3.9 broadcast_select_fusion
  19.0 243.4 %all-reduce.3.cloned.1.call-done = (f32[1,512,512]{2,1,0:T(8,128)}, f32[1,512,512]{2,1,0:T(8,128)}, f32[1,512,512]{2,1,0:T(8,128)}, f32[1,512,512]{2,1,0:T(8,128...) async-done(((f32[1,512,512]{2,1,0:T(8,128)}, f32[1,512,512]{2,1,0:T(8,128)}, f32[1,512,512]{2,1,0:T(8,128)}, f32[1,512,512]{2,1,0:T(8,128)}, f32[1,512,512]{2,1,0:T(8,128)}, ...) | async-done | bytes 6291472 | tf_op jit(solution)/shard_map/psum | solution.py:9
  262.4 2.4 constant_dynamic-update-slice_fusion.5
  264.9 2.3 constant_dynamic-update-slice_fusion.4
  267.2 2.3 constant_dynamic-update-slice_fusion.3
  272.7 4.6 conditional.4
  277.3 207.5 %while.20 = (s32[]{:T(128)}, f32[1024,256]{1,0:T(8,128)S(1)}, f32[512,256]{1,0:T(8,128)S(1)}, s32[6]{0:T(128)S(1)}, f32[6,512,512]{2,1,0:T(8,128)}, /*index=5*/s32[]{:T(128)}, s32[]{:T(128)}, s32[]{:T(128)}) while((s32[]{:T(128)}, f32[1024,256]{1,0:T(8,128)S(1)}, f32[512,256]{1,0:T(8,128)S(1)}, s32[6]{0:T(128)S(1)}, ...), condition=%wide.region_23.24_spmd.clone.clone, body=%wide.region_14.23_spmd.clone.clone.sunk | while | flops 1610874880 | bytes 11534837 | solution.py:60
  280.1 25.7 %collective-permute-done = f32[1024,256]{1,0:T(8,128)S(1)} collective-permute-done((f32[1024,256]{1,0:T(8,128)S(1)}, f32[1024,256]{1,0:T(8,128)S(1)}, u32[]{:S(2)}, u32[]{:S(2)}) %collective-permute-start) | collective-permute-done | bytes 1048608 | tf_op jit(solution)/shard_map/while/body/eval_jaxpr/ppermute | solution.py:14
  305.8 5.0 %conditional.13 = (f32[512,256]{1,0:T(8,128)S(1)}) conditional(s32[]{:T(128)} %convert_element_type.28, f32[512,256]{1,0:T(8,128)S(1)} %get-tuple-element.519, (pred[6]{0:T(512)(128)(4,1)S(1)}, s32[6]{0:T(128)S(1)}, f32[6,512,512]{2,1,0:T(8,128)}, f32[1024,256]{1,0:T(8,128)S(1)}, f32[512,256]{1,0:T(8,128)S(1)}) %tuple.109), branch_computations={%region_20.20_spmd, %region_21.22_spmd} | conditional | flops 805437440 | bytes 2621520 | solution.py:50
  308.4 2.4 convolution_add_fusion.1
  312.9 25.7 %collective-permute-done = f32[1024,256]{1,0:T(8,128)S(1)} collective-permute-done((f32[1024,256]{1,0:T(8,128)S(1)}, f32[1024,256]{1,0:T(8,128)S(1)}, u32[]{:S(2)}, u32[]{:S(2)}) %collective-permute-start) | collective-permute-done | bytes 1048608 | tf_op jit(solution)/shard_map/while/body/eval_jaxpr/ppermute | solution.py:14
  338.6 5.0 %conditional.13 = (f32[512,256]{1,0:T(8,128)S(1)}) conditional(s32[]{:T(128)} %convert_element_type.28, f32[512,256]{1,0:T(8,128)S(1)} %get-tuple-element.519, (pred[6]{0:T(512)(128)(4,1)S(1)}, s32[6]{0:T(128)S(1)}, f32[6,512,512]{2,1,0:T(8,128)}, f32[1024,256]{1,0:T(8,128)S(1)}, f32[512,256]{1,0:T(8,128)S(1)}) %tuple.109), branch_computations={%region_20.20_spmd, %region_21.22_spmd} | conditional | flops 805437440 | bytes 2621520 | solution.py:50
  341.2 2.4 convolution_add_fusion.1
  345.7 24.8 %collective-permute-done = f32[1024,256]{1,0:T(8,128)S(1)} collective-permute-done((f32[1024,256]{1,0:T(8,128)S(1)}, f32[1024,256]{1,0:T(8,128)S(1)}, u32[]{:S(2)}, u32[]{:S(2)}) %collective-permute-start) | collective-permute-done | bytes 1048608 | tf_op jit(solution)/shard_map/while/body/eval_jaxpr/ppermute | solution.py:14
  372.6 24.0 %collective-permute-done = f32[1024,256]{1,0:T(8,128)S(1)} collective-permute-done((f32[1024,256]{1,0:T(8,128)S(1)}, f32[1024,256]{1,0:T(8,128)S(1)}, u32[]{:S(2)}, u32[]{:S(2)}) %collective-permute-start) | collective-permute-done | bytes 1048608 | tf_op jit(solution)/shard_map/while/body/eval_jaxpr/ppermute | solution.py:14
  396.6 5.0 %conditional.13 = (f32[512,256]{1,0:T(8,128)S(1)}) conditional(s32[]{:T(128)} %convert_element_type.28, f32[512,256]{1,0:T(8,128)S(1)} %get-tuple-element.519, (pred[6]{0:T(512)(128)(4,1)S(1)}, s32[6]{0:T(128)S(1)}, f32[6,512,512]{2,1,0:T(8,128)}, f32[1024,256]{1,0:T(8,128)S(1)}, f32[512,256]{1,0:T(8,128)S(1)}) %tuple.109), branch_computations={%region_20.20_spmd, %region_21.22_spmd} | conditional | flops 805437440 | bytes 2621520 | solution.py:50
  399.1 2.4 convolution_add_fusion.1
  403.7 23.1 %collective-permute-done = f32[1024,256]{1,0:T(8,128)S(1)} collective-permute-done((f32[1024,256]{1,0:T(8,128)S(1)}, f32[1024,256]{1,0:T(8,128)S(1)}, u32[]{:S(2)}, u32[]{:S(2)}) %collective-permute-start) | collective-permute-done | bytes 1048608 | tf_op jit(solution)/shard_map/while/body/eval_jaxpr/ppermute | solution.py:14
  428.9 22.2 %collective-permute-done = f32[1024,256]{1,0:T(8,128)S(1)} collective-permute-done((f32[1024,256]{1,0:T(8,128)S(1)}, f32[1024,256]{1,0:T(8,128)S(1)}, u32[]{:S(2)}, u32[]{:S(2)}) %collective-permute-start) | collective-permute-done | bytes 1048608 | tf_op jit(solution)/shard_map/while/body/eval_jaxpr/ppermute | solution.py:14
  451.1 5.0 %conditional.12 = (f32[512,256]{1,0:T(8,128)S(1)}) conditional(s32[]{:T(128)} %convert_element_type.29, f32[512,256]{1,0:T(8,128)S(1)} %get-tuple-element.497, (f32[6,512,512]{2,1,0:T(8,128)}, f32[1024,256]{1,0:T(8,128)S(1)}, f32[512,256]{1,0:T(8,128)S(1)}, pred[6]{0:T(512)(128)(4,1)S(1)}, s32[]{:T(128)}, /*index=5*/s32[]{:T(128)}, ...), branch_computations={%region_18.18_spmd, %region_19.19_spmd.clone.clone} | conditional | flops 805437440 | bytes 2621528 | solution.py:50
  453.7 2.4 convolution_add_fusion.2
  458.3 21.4 %collective-permute-done = f32[1024,256]{1,0:T(8,128)S(1)} collective-permute-done((f32[1024,256]{1,0:T(8,128)S(1)}, f32[1024,256]{1,0:T(8,128)S(1)}, u32[]{:S(2)}, u32[]{:S(2)}) %collective-permute-start) | collective-permute-done | bytes 1048608 | tf_op jit(solution)/shard_map/while/body/eval_jaxpr/ppermute | solution.py:14
  479.7 5.0 %conditional.13 = (f32[512,256]{1,0:T(8,128)S(1)}) conditional(s32[]{:T(128)} %convert_element_type.28, f32[512,256]{1,0:T(8,128)S(1)} %get-tuple-element.519, (pred[6]{0:T(512)(128)(4,1)S(1)}, s32[6]{0:T(128)S(1)}, f32[6,512,512]{2,1,0:T(8,128)}, f32[1024,256]{1,0:T(8,128)S(1)}, f32[512,256]{1,0:T(8,128)S(1)}) %tuple.109), branch_computations={%region_20.20_spmd, %region_21.22_spmd} | conditional | flops 805437440 | bytes 2621520 | solution.py:50
  482.2 2.4 convolution_add_fusion.1
  (66 shorter events, 20.6 us)
Async XLA Ops:
  6.5 255.9 %all-reduce.3.cloned.1.call-start = ((), (), s32[]{:S(2)}) async-start(), calls=%async_computation | async-start | bytes 12582912 | tf_op jit(solution)/shard_map/psum | solution.py:9
  13.1 4.0 copy-start.4
  262.4 7.0 %copy-start.2 = (f32[1,512,512]{2,1,0:T(8,128)S(1)}, f32[1,512,512]{2,1,0:T(8,128)}, u32[]{:S(2)}) copy-start(f32[1,512,512]{2,1,0:T(8,128)} %get-tuple-element.425) | copy-start | bytes 3145732
  262.4 8.1 %copy-start.1 = (f32[1,512,512]{2,1,0:T(8,128)S(1)}, f32[1,512,512]{2,1,0:T(8,128)}, u32[]{:S(2)}) copy-start(f32[1,512,512]{2,1,0:T(8,128)} %get-tuple-element.426) | copy-start | bytes 3145732
  262.4 9.1 %copy-start = (f32[1,512,512]{2,1,0:T(8,128)S(1)}, f32[1,512,512]{2,1,0:T(8,128)}, u32[]{:S(2)}) copy-start(f32[1,512,512]{2,1,0:T(8,128)} %get-tuple-element.427) | copy-start | bytes 3145732
  277.3 207.5 %copy-start.3 = (f32[512,256]{1,0:T(8,128)S(1)}, f32[512,256]{1,0:T(8,128)}, u32[]{:S(2)}) copy-start(f32[512,256]{1,0:T(8,128)} %param.17) | copy-start | bytes 1572868
  277.3 28.5 %collective-permute-start = (f32[1024,256]{1,0:T(8,128)S(1)}, f32[1024,256]{1,0:T(8,128)S(1)}, u32[]{:S(2)}, u32[]{:S(2)}) collective-permute-start(f32[1024,256]{1,0:T(8,128)S(1)} %get-tuple-element.496), channel_id=1, source_target_pairs={{0,7},{1,0},{2,1},{3,2},{4,3},{5,4},{6,5},{7,6},{8,15},{9,8},{10,9... | collective-permute-start | bytes 3145736 | tf_op jit(solution)/shard_map/while/body/eval_jaxpr/ppermute | solution.py:14
  310.9 27.7 %collective-permute-start = (f32[1024,256]{1,0:T(8,128)S(1)}, f32[1024,256]{1,0:T(8,128)S(1)}, u32[]{:S(2)}, u32[]{:S(2)}) collective-permute-start(f32[1024,256]{1,0:T(8,128)S(1)} %get-tuple-element.496), channel_id=1, source_target_pairs={{0,7},{1,0},{2,1},{3,2},{4,3},{5,4},{6,5},{7,6},{8,15},{9,8},{10,9... | collective-permute-start | bytes 3145736 | tf_op jit(solution)/shard_map/while/body/eval_jaxpr/ppermute | solution.py:14
  343.7 26.8 %collective-permute-start = (f32[1024,256]{1,0:T(8,128)S(1)}, f32[1024,256]{1,0:T(8,128)S(1)}, u32[]{:S(2)}, u32[]{:S(2)}) collective-permute-start(f32[1024,256]{1,0:T(8,128)S(1)} %get-tuple-element.496), channel_id=1, source_target_pairs={{0,7},{1,0},{2,1},{3,2},{4,3},{5,4},{6,5},{7,6},{8,15},{9,8},{10,9... | collective-permute-start | bytes 3145736 | tf_op jit(solution)/shard_map/while/body/eval_jaxpr/ppermute | solution.py:14
  370.6 26.0 %collective-permute-start = (f32[1024,256]{1,0:T(8,128)S(1)}, f32[1024,256]{1,0:T(8,128)S(1)}, u32[]{:S(2)}, u32[]{:S(2)}) collective-permute-start(f32[1024,256]{1,0:T(8,128)S(1)} %get-tuple-element.496), channel_id=1, source_target_pairs={{0,7},{1,0},{2,1},{3,2},{4,3},{5,4},{6,5},{7,6},{8,15},{9,8},{10,9... | collective-permute-start | bytes 3145736 | tf_op jit(solution)/shard_map/while/body/eval_jaxpr/ppermute | solution.py:14
  401.7 25.1 %collective-permute-start = (f32[1024,256]{1,0:T(8,128)S(1)}, f32[1024,256]{1,0:T(8,128)S(1)}, u32[]{:S(2)}, u32[]{:S(2)}) collective-permute-start(f32[1024,256]{1,0:T(8,128)S(1)} %get-tuple-element.496), channel_id=1, source_target_pairs={{0,7},{1,0},{2,1},{3,2},{4,3},{5,4},{6,5},{7,6},{8,15},{9,8},{10,9... | collective-permute-start | bytes 3145736 | tf_op jit(solution)/shard_map/while/body/eval_jaxpr/ppermute | solution.py:14
  426.9 24.3 %collective-permute-start = (f32[1024,256]{1,0:T(8,128)S(1)}, f32[1024,256]{1,0:T(8,128)S(1)}, u32[]{:S(2)}, u32[]{:S(2)}) collective-permute-start(f32[1024,256]{1,0:T(8,128)S(1)} %get-tuple-element.496), channel_id=1, source_target_pairs={{0,7},{1,0},{2,1},{3,2},{4,3},{5,4},{6,5},{7,6},{8,15},{9,8},{10,9... | collective-permute-start | bytes 3145736 | tf_op jit(solution)/shard_map/while/body/eval_jaxpr/ppermute | solution.py:14
  456.3 23.4 %collective-permute-start = (f32[1024,256]{1,0:T(8,128)S(1)}, f32[1024,256]{1,0:T(8,128)S(1)}, u32[]{:S(2)}, u32[]{:S(2)}) collective-permute-start(f32[1024,256]{1,0:T(8,128)S(1)} %get-tuple-element.496), channel_id=1, source_target_pairs={{0,7},{1,0},{2,1},{3,2},{4,3},{5,4},{6,5},{7,6},{8,15},{9,8},{10,9... | collective-permute-start | bytes 3145736 | tf_op jit(solution)/shard_map/while/body/eval_jaxpr/ppermute | solution.py:14
Sparse Core Ops, SparseCore 0:
  17.2 245.1 all-reduce.2
where the time goes:
time: 501 us; the launch traced here: 492 us
  waiting for transfers between devices  410 us (82%)
  loops' own time  20.1 us (4%)
  between operations  18.5 us (4%)
  other arithmetic  14.4 us (3%)
  matrix products  14.3 us (3%)
  local copies, waits for them, and re-layouts  13.5 us (3%)
    psum x1, waiting for transfers between devices, spread(): return lax.psum(jnp.where(mine, array, jnp.zeros_like(array)), axis)  243 us
    ppermute x7, waiting for transfers between devices, from_behind(): lax.ppermute(array, axis, [(i, (i + by) % peers) for i in range(peers)])  167 us
    dot_general x6, matrix products, multiply(): jnp.dot(left_block, right_block, precision=lax.Precision.HIGHEST, preferr...  14.3 us
    another operation x16, loops' own time, add_step(): accum = lax.cond(present, with_block, without_block, accum)  11.3 us
    unnamed x16, local copies, waits for them, and re-layouts  10.4 us
  transfers between devices with their start and end apart: 8, of which 8 were waited for; matrix products, arithmetic and copies ran while one was open for 1% of the time, Pallas kernels for 0%

commit v1 on v0

v1 whole, which is shorter than its diff:
```python
import functools

import jax
import jax.numpy as jnp
from jax import lax
from jax.experimental import pallas as pl
from jax.experimental.pallas import tpu as pltpu
from jax.sharding import PartitionSpec as P

NY, NZ, NC = 2, 8, 2
NROW = NY * NZ * NC
NH, NX = 2, 4
ND = 6
KW = 512
COLS = 256
CH = KW // NROW
QUAD = NY * NC * CH
HALF = ND // 2


def chunk_of(zz, yy, cc):
    return (zz * NY + yy) * NC + cc


def row_of(zz, yy, cc):
    return (yy * NZ + zz) * NC + cc


def kernel(
    offsets,
    owners,
    left,
    right,
    out,
    spread,
    chosen,
    partner_chosen,
    gathered,
    rights,
    right_hi,
    right_lo,
    own_sum,
    other_sum,
    send_par,
    recv_par,
    spread_send,
    spread_recv,
    swap_sem,
    right_send,
    right_recv,
    local_sem,
    gather_send,
    gather_recv,
    par_send,
    par_recv,
):
    row = lax.axis_index("row")
    col = lax.axis_index("col")
    y = row // (NZ * NC)
    z = (row // NC) % NZ
    c = row % NC
    h = col // NX
    x = col % NX
    mine = chunk_of(z, y, c)
    east = h * NX + (x + 1) % NX
    west = h * NX + (x + NX - 1) % NX
    partner = (1 - h) * NX + x

    barrier = pltpu.get_barrier_semaphore()

    def greet(step, carry):
        pl.semaphore_signal(barrier, inc=1, device_id={"row": (row + step) % NROW})
        return carry

    lax.fori_loop(1, NROW, greet, 0)
    for where in (east, west, partner):
        pl.semaphore_signal(barrier, inc=1, device_id={"col": where})
    pl.semaphore_wait(barrier, NROW - 1 + 3)

    def right_copy(source_ref, owner, slot, way, where):
        return pltpu.make_async_remote_copy(
            src_ref=source_ref,
            dst_ref=rights.at[owner, slot],
            send_sem=right_send.at[way, slot],
            recv_sem=right_recv.at[owner, slot],
            device_id={"col": where},
        )

    first = []
    for slot_east, slot_west in ((0, 1), (1, 0)):
        for way, slot, where in ((0, slot_east, east), (1, slot_west, west)):
            copy = right_copy(right.at[slot], x, slot, way, where)
            copy.start()
            first.append(copy)

    def spread_copy(step):
        peer = (row + step) % NROW
        py = peer // (NZ * NC)
        pz = (peer // NC) % NZ
        pc = peer % NC
        begin = pl.multiple_of(chunk_of(pz, py, pc) * CH, CH)
        return pltpu.make_async_remote_copy(
            src_ref=left.at[pl.ds(begin, CH)],
            dst_ref=spread.at[row],
            send_sem=spread_send.at[step],
            recv_sem=spread_recv.at[row],
            device_id={"row": peer},
        )

    def spread_start(step, carry):
        spread_copy(step).start()
        return carry

    lax.fori_loop(1, NROW, spread_start, 0)
    local = pltpu.make_async_copy(right, rights.at[x], local_sem.at[0])
    local.start()
    own_begin = pl.multiple_of(mine * CH, CH)
    spread[row] = left[pl.ds(own_begin, CH), :]

    def spread_done(step, carry):
        peer = (row + step) % NROW
        pltpu.make_async_remote_copy(
            src_ref=spread.at[peer],
            dst_ref=spread.at[peer],
            send_sem=spread_send.at[step],
            recv_sem=spread_recv.at[peer],
            device_id={"row": peer},
        ).wait_recv()
        return carry

    lax.fori_loop(1, NROW, spread_done, 0)

    for number in range(ND):
        chosen[number] = spread[owners[0, number]]
    swap = pltpu.make_async_remote_copy(
        src_ref=chosen,
        dst_ref=partner_chosen,
        send_sem=swap_sem.at[0],
        recv_sem=swap_sem.at[1],
        device_id={"col": partner},
    )
    swap.start()
    shift = [offsets[number] // 2 for number in range(ND)]
    parity = [offsets[number] % 2 for number in range(ND)]
    crossed = [((x + shift[number]) // NX) % 2 for number in range(ND)]
    swap.wait_recv()
    for number in range(ND):
        gathered[mine, number] = jnp.where(
            crossed[number] == 1, partner_chosen[number], chosen[number]
        )

    beside = {"row": row_of(z, y, 1 - c)}
    across = {"row": row_of(z, 1 - y, c)}
    up = {"row": row_of((z + 1) % NZ, y, c)}
    down = {"row": row_of((z + NZ - 1) % NZ, y, c)}
    BESIDE, ACROSS, UP, DOWN = 0, 1, 2, 3
    targets = {BESIDE: beside, ACROSS: across, UP: up, DOWN: down}
    sent = {BESIDE: 0, ACROSS: 0, UP: 0, DOWN: 0}

    def unit_copy(zz, yy, cc, part, way):
        chunk = chunk_of(zz, yy, cc)
        ref = gathered.at[chunk, pl.ds(part * HALF, HALF)]
        return pltpu.make_async_remote_copy(
            src_ref=ref,
            dst_ref=ref,
            send_sem=gather_send.at[way],
            recv_sem=gather_recv.at[chunk, part],
            device_id=targets[way],
        )

    def send(zz, yy, cc, part, *ways):
        for way in ways:
            sent[way] += 1
            unit_copy(zz, yy, cc, part, way).start()

    def receive(zz, yy, cc, part):
        unit_copy(zz, yy, cc, part, BESIDE).wait_recv()

    send(z, y, c, 0, ACROSS, UP, DOWN)
    send(z, y, c, 1, UP, DOWN, ACROSS)
    send(z, y, c, 0, BESIDE)
    send(z, y, c, 1, BESIDE)
    receive(z, 1 - y, c, 0)
    send(z, 1 - y, c, 0, UP, DOWN, BESIDE)

    def right_wait(owner, slot):
        right_copy(rights.at[owner, slot], owner, slot, 0, east).wait_recv()

    x_west = (x + NX - 1) % NX
    x_east = (x + 1) % NX
    x_far = (x + 2) % NX
    right_wait(x_west, 0)
    relay_east = right_copy(rights.at[x_west, 0], x_west, 0, 2, east)
    relay_east.start()
    right_wait(x_east, 1)
    relay_west = right_copy(rights.at[x_east, 1], x_east, 1, 2, west)
    relay_west.start()

    def z_stage(step):
        below = (z + NZ - step) % NZ
        above = (z + step) % NZ
        far = step == NZ // 2
        last = step == NZ // 2 - 1
        todo = []
        for yy, part in ((y, 0), (y, 1), (1 - y, 0)):
            extra = (ACROSS, BESIDE) if part == 1 else (BESIDE,)
            if not (far and part == 1):
                on = () if far or (last and part == 1) else (UP,)
                todo.append((below, yy, part, on + extra))
            if not (far and part == 0):
                on = () if far or (last and part == 0) else (DOWN,)
                todo.append((above, yy, part, on + extra))
        for zz, yy, part, ways in todo:
            receive(zz, yy, c, part)
            send(zz, yy, c, part, *ways)

    def places(step):
        if step == 0:
            return (z,)
        if step == NZ // 2:
            return ((z + step) % NZ,)
        return ((z + NZ - step) % NZ, (z + step) % NZ)

    def y_stage(step):
        for zz in places(step):
            receive(zz, 1 - y, c, 1)
            send(zz, 1 - y, c, 1, BESIDE)

    def par_copy(zz):
        return pltpu.make_async_remote_copy(
            src_ref=send_par.at[zz],
            dst_ref=recv_par.at[zz],
            send_sem=par_send.at[zz],
            recv_sem=par_recv.at[zz],
            device_id={"col": partner},
        )

    def multiply_stage(step):
        spots = places(step)
        for zz in spots:
            for yy in (0, 1):
                for part in (0, 1):
                    receive(zz, yy, 1 - c, part)
        rows = QUAD * len(spots)
        for number in range(ND):
            pieces = []
            for zz in spots:
                begin = zz * NY * NC
                pieces.append(
                    gathered[pl.ds(begin, NY * NC), number].reshape(QUAD, KW)
                )
            block = pieces[0] if len(pieces) == 1 else jnp.concatenate(pieces, axis=0)
            hi = block.astype(jnp.bfloat16)
            lo = (block - hi.astype(jnp.float32)).astype(jnp.bfloat16)
            rhi = right_hi[number]
            rlo = right_lo[number]
            term = jnp.dot(hi, rhi, preferred_element_type=jnp.float32)
            term += jnp.dot(hi, rlo, preferred_element_type=jnp.float32)
            term += jnp.dot(lo, rhi, preferred_element_type=jnp.float32)
            zero = jnp.zeros_like(term)
            other = jnp.where(crossed[number] == 1, term, zero)
            here = jnp.where(crossed[number] == 1, zero, term)
            if number == 0:
                own_sum[pl.ds(0, rows)] = here
                other_sum[pl.ds(0, rows)] = other
            else:
                own_sum[pl.ds(0, rows)] += here
                other_sum[pl.ds(0, rows)] += other
        for index, zz in enumerate(spots):
            send_par[zz] = other_sum[index * QUAD : (index + 1) * QUAD]
            par_copy(zz).start()
            begin = pl.multiple_of(zz * QUAD, QUAD)
            out[pl.ds(begin, QUAD)] = own_sum[index * QUAD : (index + 1) * QUAD]

    def finish_stage(step):
        for zz in places(step):
            par_copy(zz).wait_recv()
            begin = pl.multiple_of(zz * QUAD, QUAD)
            out[pl.ds(begin, QUAD)] += recv_par[zz]

    def prepare_right():
        local.wait()
        right_wait(x_west, 1)
        right_wait(x_east, 0)
        right_wait(x_far, 0)
        right_wait(x_far, 1)
        for number in range(ND):
            block = rights[(x + shift[number]) % NX, parity[number]]
            hi = block.astype(jnp.bfloat16)
            right_hi[number] = hi
            right_lo[number] = (block - hi.astype(jnp.float32)).astype(jnp.bfloat16)

    z_stage(1)
    y_stage(0)
    z_stage(2)
    y_stage(1)
    z_stage(3)
    prepare_right()
    y_stage(2)
    multiply_stage(0)
    multiply_stage(1)
    z_stage(4)
    y_stage(3)
    multiply_stage(2)
    finish_stage(0)
    finish_stage(1)
    y_stage(4)
    multiply_stage(3)
    finish_stage(2)
    multiply_stage(4)
    finish_stage(3)
    finish_stage(4)

    def spread_sent(step, carry):
        spread_copy(step).wait_send()
        return carry

    lax.fori_loop(1, NROW, spread_sent, 0)
    for copy in first + [relay_east, relay_west, swap]:
        copy.wait_send()
    for zz in range(NZ):
        par_copy(zz).wait_send()
    for way in targets:
        ref = gathered.at[pl.ds(0, sent[way]), pl.ds(0, HALF)]
        pltpu.make_async_remote_copy(
            src_ref=ref,
            dst_ref=ref,
            send_sem=gather_send.at[way],
            recv_sem=gather_recv.at[0, 0],
            device_id=targets[way],
        ).wait_send()


def shards(left_slots, right, previous, offsets, owners):
    f32 = jnp.float32
    vmem = pl.BlockSpec(memory_space=pltpu.VMEM)
    smem = pl.BlockSpec(memory_space=pltpu.SMEM)
    dma = pltpu.SemaphoreType.DMA
    total = pl.pallas_call(
        kernel,
        out_shape=jax.ShapeDtypeStruct((KW, COLS), f32),
        in_specs=[smem, smem, vmem, vmem],
        out_specs=vmem,
        scratch_shapes=[
            pltpu.VMEM((NROW, CH, KW), f32),
            pltpu.VMEM((ND, CH, KW), f32),
            pltpu.VMEM((ND, CH, KW), f32),
            pltpu.VMEM((NROW, ND, CH, KW), f32),
            pltpu.VMEM((NX, 2, KW, COLS), f32),
            pltpu.VMEM((ND, KW, COLS), jnp.bfloat16),
            pltpu.VMEM((ND, KW, COLS), jnp.bfloat16),
            pltpu.VMEM((2 * QUAD, COLS), f32),
            pltpu.VMEM((2 * QUAD, COLS), f32),
            pltpu.VMEM((NZ, QUAD, COLS), f32),
            pltpu.VMEM((NZ, QUAD, COLS), f32),
            dma((NROW,)),
            dma((NROW,)),
            dma((2,)),
            dma((3, 2)),
            dma((NX, 2)),
            dma((1,)),
            dma((4,)),
            dma((NROW, 2)),
            dma((NZ,)),
            dma((NZ,)),
        ],
        compiler_params=pltpu.CompilerParams(
            collective_id=0, has_side_effects=True, vmem_limit_bytes=48 * 1024 * 1024
        ),
    )(offsets, owners, left_slots[0], right.reshape(2, KW, COLS))
    return 2.0 * previous - total


def solution(mesh):
    return jax.shard_map(
        shards,
        mesh=mesh,
        in_specs=(P("row", "col", None), P("col", "row"), P("col", "row"), P(), P("col", None)),
        out_specs=P("col", "row"),
        check_vma=False,
    )
```

time: 501 us -> 89.1 us (0.18); the launches traced: 492 us -> 88.9 us
  waiting for transfers between devices: 410 us -> 0 us
  Pallas kernels: 0 us -> 84.9 us
  loops' own time: 20.1 us -> 0 us
  between operations: 18.5 us -> 0.02 us
  matrix products: 14.3 us -> 0 us
  other arithmetic: 14.4 us -> 0.86 us
  local copies, waits for them, and re-layouts: 13.5 us -> 3.12 us
    psum x1 -> x0, waiting for transfers between devices: 243 us -> none  [spread(): return lax.psum(jnp.where(mine, array, jnp.zeros_like(array)), axis)]
    ppermute x7 -> x0, waiting for transfers between devices: 167 us -> none  [from_behind(): lax.ppermute(array, axis, [(i, (i + by) % peers) for i in range(peers)])]
    pallas_call x0 -> x1, Pallas kernels: none -> 84.9 us  [shards(): pl.pallas_call(kernel, out_shape=jax.ShapeDtypeStruct((KW, COLS), f32), i...]
    another operation x17 -> x0, loops' own time: 20.1 us -> none  [the longest x16 11.3 us: add_step(): accum = lax.cond(present, with_block, without_block, accum)]
    dot_general x6 -> x0, matrix products: 14.3 us -> none  [multiply(): jnp.dot(left_block, right_block, precision=lax.Precision.HIGHEST, preferr...]
    unnamed x16 -> x10, local copies, waits for them, and re-layouts: 10.4 us -> 3.12 us
    reduce_or x8 -> x0, other arithmetic: 5.61 us -> none  [add_step(): present = jnp.any(matched)]
  transfers between devices with their start and end apart: 8 -> 0, of which waited for: 8 -> 0; matrix products, arithmetic and copies ran while one was open for 1% -> 0% of each run, Pallas kernels for 0% -> 0%
where the time goes in v1:
time: 89.1 us; the launch traced here: 88.9 us
  Pallas kernels  84.9 us (95%)
  local copies, waits for them, and re-layouts  3.12 us (4%)
    pallas_call x1, Pallas kernels, shards(): pl.pallas_call(kernel, out_shape=jax.ShapeDtypeStruct((KW, COLS), f32), i...  84.9 us
    unnamed x10, local copies, waits for them, and re-layouts  3.12 us

profile of v1, /device:TPU:6, one launch (start us, length us, event | category | flops | bytes accessed | tf_op | source)
XLA Modules:
  0.0 88.9 jit_solution(4617223741870279349)
XLA Ops:
  0.0 0.0 copy-start.2
  0.0 0.0 copy-start.3
  0.0 0.7 copy-done.2
  0.7 0.0 copy-done.3
  0.7 0.0 copy-start
  0.7 1.2 %copy-done = f32[1,512,512]{2,1,0:T(8,128)S(1)} copy-done((f32[1,512,512]{2,1,0:T(8,128)S(1)}, f32[1,512,512]{2,1,0:T(8,128)}, u32[]{:S(2)}) %copy-start) | copy-done | bytes 1048600
  1.9 0.0 copy-start.1
  1.9 1.2 %copy-done.1 = f32[1024,256]{1,0:T(8,128)S(1)} copy-done((f32[1024,256]{1,0:T(8,128)S(1)}, f32[1024,256]{1,0:T(8,128)}, u32[]{:S(2)}) %copy-start.1) | copy-done | bytes 1048600
  3.1 0.0 copy-start.4
  3.1 84.9 %shard_map.55 = f32[512,256]{1,0:T(8,128)S(1)} custom-call(s32[6]{0:T(128)S(1)} %copy-done.2, s32[1,6]{1,0:T(1,128)S(1)} %copy-done.3, f32[512,512]{1,0:T(8,128)S(1)} %bitcast.2, f32[2,512,256]{2,1,0:T(8,128)S(1)} %bitcast.3), custom_call_target="tpu_custom_call" | custom-call | tf_op jit(solution)/shard_map/pallas_call | solution.py:339
  88.0 0.0 copy-done.4
  88.1 0.9 multiply_subtract_fusion
Async XLA Ops:
  0.0 0.7 copy-start.2
  0.0 0.7 copy-start.3
  0.7 1.2 %copy-start = (f32[1,512,512]{2,1,0:T(8,128)S(1)}, f32[1,512,512]{2,1,0:T(8,128)}, u32[]{:S(2)}) copy-start(f32[1,512,512]{2,1,0:T(8,128)} %param.5) | copy-start | bytes 3145732
  1.9 1.2 %copy-start.1 = (f32[1024,256]{1,0:T(8,128)S(1)}, f32[1024,256]{1,0:T(8,128)}, u32[]{:S(2)}) copy-start(f32[1024,256]{1,0:T(8,128)} %param.6) | copy-start | bytes 3145732
  3.1 84.9 %copy-start.4 = (f32[512,256]{1,0:T(8,128)S(1)}, f32[512,256]{1,0:T(8,128)}, u32[]{:S(2)}) copy-start(f32[512,256]{1,0:T(8,128)} %param.7) | copy-start | bytes 1572868

commit v2 on v0

v2 whole, which is shorter than its diff:
```python
import jax
import jax.numpy as jnp
from jax import lax
from jax.experimental import pallas as pl
from jax.experimental.pallas import tpu as pltpu
from jax.sharding import PartitionSpec as P

NY, NZ, NC = 2, 8, 2
NROW = NY * NZ * NC
NH, NX = 2, 4
ND = 6
KW = 512
COLS = 256
PARTS = 2
CH = KW // NROW // PARTS
QUAD = NY * NC * CH
SPAN = NZ * QUAD
HALF = ND // 2


def chunk_of(zz, yy, cc):
    return (zz * NY + yy) * NC + cc


def row_of(zz, yy, cc):
    return (yy * NZ + zz) * NC + cc


def kernel(
    offsets_hbm,
    owners_hbm,
    left,
    right,
    out,
    offsets,
    owners,
    spread_first,
    spread_second,
    chosen,
    partner_chosen,
    gathered,
    rights,
    right_hi,
    right_lo,
    own_sum,
    send_par,
    recv_par,
    spread_send,
    spread_recv,
    swap_send,
    swap_recv,
    right_send,
    right_recv,
    local_sem,
    gather_send,
    gather_recv,
    par_send,
    par_recv,
):
    spread = (spread_first, spread_second)
    row = lax.axis_index("row")
    col = lax.axis_index("col")
    y = row // (NZ * NC)
    z = (row // NC) % NZ
    c = row % NC
    h = col // NX
    x = col % NX
    mine = chunk_of(z, y, c)
    east = h * NX + (x + 1) % NX
    west = h * NX + (x + NX - 1) % NX
    partner = (1 - h) * NX + x
    x_west = (x + NX - 1) % NX
    x_east = (x + 1) % NX
    x_far = (x + 2) % NX

    local_right = pltpu.make_async_copy(right, rights.at[x], local_sem.at[0])
    local_right.start()
    tables = []
    for number, (source, target) in enumerate(((offsets_hbm, offsets), (owners_hbm, owners))):
        copy = pltpu.make_async_copy(source, target, local_sem.at[1 + PARTS + number])
        copy.start()
        tables.append(copy)
    local_left = []
    for part in range(PARTS):
        begin = pl.multiple_of(part * SPAN + mine * CH, CH)
        copy = pltpu.make_async_copy(
            left.at[0, pl.ds(begin, CH)], spread[part].at[row], local_sem.at[1 + part]
        )
        copy.start()
        local_left.append(copy)

    barrier = pltpu.get_barrier_semaphore()

    def greet(step, carry):
        pl.semaphore_signal(barrier, inc=1, device_id={"row": (row + step) % NROW})
        return carry

    lax.fori_loop(1, NROW, greet, 0)
    for where in (east, west, partner):
        pl.semaphore_signal(barrier, inc=1, device_id={"col": where})
    pl.semaphore_wait(barrier, NROW - 1 + 3)

    def right_copy(source_ref, owner, slot, way, where):
        return pltpu.make_async_remote_copy(
            src_ref=source_ref,
            dst_ref=rights.at[owner, slot],
            send_sem=right_send.at[way, slot],
            recv_sem=right_recv.at[owner, slot],
            device_id={"col": where},
        )

    def right_wait(owner, slot):
        right_copy(rights.at[owner, slot], owner, slot, 0, east).wait_recv()

    first = []
    for slot_east, slot_west in ((0, 1), (1, 0)):
        for way, slot, where in ((0, slot_east, east), (1, slot_west, west)):
            copy = right_copy(right.at[slot], x, slot, way, where)
            first.append(copy)

    place = y * NZ + z

    def spread_to(part, spot, cc):
        yy = spot // NZ
        zz = spot % NZ
        begin = pl.multiple_of(part * SPAN + chunk_of(zz, yy, cc) * CH, CH)
        pltpu.make_async_remote_copy(
            src_ref=left.at[0, pl.ds(begin, CH)],
            dst_ref=spread[part].at[row],
            send_sem=spread_send.at[part],
            recv_sem=spread_recv.at[part],
            device_id={"row": row_of(zz, yy, cc)},
        ).start()

    def spread_stage(part, cc):
        def spread_start(step, carry):
            spread_to(part, (place + step) % (NY * NZ), cc)
            return carry

        lax.fori_loop(1, NY * NZ, spread_start, 0)

        @pl.when(c != cc)
        def _():
            spread_to(part, place, cc)

    def spread_all(part):
        ref = spread[part].at[pl.ds(0, NROW - 1)]
        return pltpu.make_async_remote_copy(
            src_ref=ref,
            dst_ref=ref,
            send_sem=spread_send.at[part],
            recv_sem=spread_recv.at[part],
            device_id={"col": partner},
        )

    def swap_copy(part):
        return pltpu.make_async_remote_copy(
            src_ref=chosen.at[part],
            dst_ref=partner_chosen.at[part],
            send_sem=swap_send.at[part],
            recv_sem=swap_recv.at[part],
            device_id={"col": partner},
        )

    def crossing(number):
        return ((x + offsets[number] // 2) // NX) % 2

    def choose_stage(part):
        local_left[part].wait()
        spread_all(part).wait_recv()
        for number in range(ND):
            chosen[part, number] = spread[part][owners[0, number]]
        swap_copy(part).start()

    beside = {"row": row_of(z, y, 1 - c)}
    across = {"row": row_of(z, 1 - y, c)}
    up = {"row": row_of((z + 1) % NZ, y, c)}
    down = {"row": row_of((z + NZ - 1) % NZ, y, c)}
    BESIDE, ACROSS, UP, DOWN = 0, 1, 2, 3
    targets = {BESIDE: beside, ACROSS: across, UP: up, DOWN: down}
    sent = [{way: 0 for way in targets} for part in range(PARTS)]

    def unit_copy(part, zz, yy, cc, half, way):
        chunk = chunk_of(zz, yy, cc)
        ref = gathered.at[part, chunk, pl.ds(half * HALF, HALF)]
        return pltpu.make_async_remote_copy(
            src_ref=ref,
            dst_ref=ref,
            send_sem=gather_send.at[part, way],
            recv_sem=gather_recv.at[part, chunk, half],
            device_id=targets[way],
        )

    def send(part, zz, yy, cc, half, *ways):
        for way in ways:
            sent[part][way] += 1
            unit_copy(part, zz, yy, cc, half, way).start()

    def receive(part, zz, yy, cc, half):
        unit_copy(part, zz, yy, cc, half, BESIDE).wait_recv()

    def open_stage(part):
        swap_copy(part).wait_recv()
        for number in range(ND):
            gathered[part, mine, number] = jnp.where(
                crossing(number) == 1, partner_chosen[part, number], chosen[part, number]
            )
        send(part, z, y, c, 0, ACROSS, UP, DOWN)
        send(part, z, y, c, 1, UP, DOWN, ACROSS)
        send(part, z, y, c, 0, BESIDE)
        send(part, z, y, c, 1, BESIDE)

    def passing(part, zz, yy, half, *ways):
        def go():
            receive(part, zz, yy, c, half)
            send(part, zz, yy, c, half, *ways)

        return go

    def neighbour_units(part):
        return [passing(part, z, 1 - y, 0, UP, DOWN, BESIDE)]

    def z_units(part, step):
        found = []
        below = (z + NZ - step) % NZ
        above = (z + step) % NZ
        far = step == NZ // 2
        last = step == NZ // 2 - 1
        units = ((y, 0), (y, 1), (1 - y, 0))
        if far:
            units += ((1 - y, 1),)
        for yy, half in units:
            extra = (ACROSS, BESIDE) if half == 1 and not far else (BESIDE,)
            if not (far and half == 1):
                on = () if far or (last and half == 1) else (UP,)
                found.append(passing(part, below, yy, half, *(on + extra)))
            if not (far and half == 0):
                on = () if far or (last and half == 0) else (DOWN,)
                found.append(passing(part, above, yy, half, *(on + extra)))
        return found

    def places(step):
        if step == 0:
            return (z,)
        if step == NZ // 2:
            return ((z + step) % NZ,)
        return ((z + NZ - step) % NZ, (z + step) % NZ)

    def y_units(part, step):
        found = []
        last = step == NZ // 2 - 1
        for number, zz in enumerate(places(step)):
            on = (DOWN,) if last and number == 1 else ()
            found.append(passing(part, zz, 1 - y, 1, *(on + (BESIDE,))))
        return found

    def prepare_right():
        local_right.wait()
        right_wait(x_west, 1)
        right_wait(x_east, 0)
        right_wait(x_far, 0)
        right_wait(x_far, 1)

        def prepare(number, carry):
            off = offsets[number]
            block = rights[(x + off // 2) % NX, off % 2]
            hi = block.astype(jnp.bfloat16)
            right_hi[number] = hi
            right_lo[number] = (block - hi.astype(jnp.float32)).astype(jnp.bfloat16)
            return carry

        lax.fori_loop(0, ND, prepare, 0)

    def par_copy(index, begin, rows):
        return pltpu.make_async_remote_copy(
            src_ref=send_par.at[pl.ds(begin, rows)],
            dst_ref=recv_par.at[pl.ds(begin, rows)],
            send_sem=par_send.at[index],
            recv_sem=par_recv.at[index],
            device_id={"col": partner},
        )

    def multiply(part, spots, begin, rows, numbers):
        if numbers[0] == 0:
            own_sum[pl.ds(begin, rows)] = jnp.zeros((rows, COLS), jnp.float32)
            send_par[pl.ds(begin, rows)] = jnp.zeros((rows, COLS), jnp.float32)

        def add_term(number, carry):
            pieces = [
                gathered[part, pl.ds(zz * NY * NC, NY * NC), number].reshape(QUAD, KW)
                for zz in spots
            ]
            block = jnp.concatenate(pieces, axis=0)
            hi = block.astype(jnp.bfloat16)
            lo = (block - hi.astype(jnp.float32)).astype(jnp.bfloat16)
            both = jnp.concatenate([hi, lo], axis=0)
            twice = jnp.dot(both, right_hi[number], preferred_element_type=jnp.float32)
            term = jnp.dot(hi, right_lo[number], preferred_element_type=jnp.float32)
            term += twice[:rows] + twice[rows:]
            zero = jnp.zeros_like(term)
            crossed = crossing(number) == 1
            own_sum[pl.ds(begin, rows)] += jnp.where(crossed, zero, term)
            send_par[pl.ds(begin, rows)] += jnp.where(crossed, term, zero)
            return carry

        lax.fori_loop(*numbers, add_term, 0)

    def wait_beside(part, spots):
        for zz in spots:
            for yy in (0, 1):
                for half in (0, 1):
                    receive(part, zz, yy, 1 - c, half)

    near = [spot for step in range(NZ // 2 - 1) for spot in places(step)]
    late = [spot for step in (NZ // 2 - 1, NZ // 2) for spot in places(step)]
    jobs = []
    for part in range(PARTS):
        for spots in (near, late):
            begin = jobs[-1][2] + jobs[-1][3] if jobs else 0
            jobs.append((part, spots, begin, len(spots) * QUAD))

    def multiply_units(job, slices=1):
        part, spots, begin, rows = jobs[job]
        size = ND // slices

        def piece(index):
            def go():
                if index == 0:
                    wait_beside(part, spots)
                multiply(part, spots, begin, rows, (index * size, index * size + size))
                if index == slices - 1:
                    par_copy(job, begin, rows).start()

            return go

        return [piece(index) for index in range(slices)]

    def run(*lists):
        longest = max(len(units) for units in lists)
        for turn in range(longest):
            for units in lists:
                first_unit = -(-turn * len(units) // longest)
                last_unit = -(-(turn + 1) * len(units) // longest)
                for unit in units[first_unit:last_unit]:
                    unit()

    def finish_stage(job):
        part, spots, begin, rows = jobs[job]
        par_copy(job, begin, rows).wait_recv()
        for number, zz in enumerate(spots):
            piece = pl.ds(begin + number * QUAD, QUAD)
            place = pl.multiple_of(part * SPAN + zz * QUAD, QUAD)
            out[pl.ds(place, QUAD)] = own_sum[piece] + recv_par[piece]

    spread_stage(0, 0)
    spread_stage(0, 1)
    for copy in first:
        copy.start()

    @pl.when(c == 1)
    def _():
        spread_stage(1, 0)

    for copy in tables:
        copy.wait()
    choose_stage(0)

    @pl.when(c == 0)
    def _():
        spread_stage(1, 0)

    spread_stage(1, 1)
    open_stage(0)
    run(neighbour_units(0))
    choose_stage(1)
    right_wait(x_west, 0)
    relay_east = right_copy(rights.at[x_west, 0], x_west, 0, 2, east)
    relay_east.start()
    right_wait(x_east, 1)
    relay_west = right_copy(rights.at[x_east, 1], x_east, 1, 2, west)
    relay_west.start()
    run(z_units(0, 1), y_units(0, 0))
    run(z_units(0, 2))
    open_stage(1)
    run(y_units(0, 1))
    run(z_units(0, 3), neighbour_units(1))
    run(y_units(0, 2))
    run(z_units(1, 1), y_units(1, 0))
    run(y_units(0, 3))
    run(z_units(1, 2), z_units(0, 4))
    run(y_units(1, 1))
    prepare_right()
    run(z_units(1, 3), multiply_units(0, 3))
    run(y_units(1, 2))
    run(y_units(1, 3), multiply_units(1, 3))
    run(multiply_units(2))
    run(z_units(1, 4))
    run(multiply_units(3))
    for job in range(len(jobs)):
        finish_stage(job)

    for copy in first + [relay_east, relay_west]:
        copy.wait_send()
    for part in range(PARTS):
        spread_all(part).wait_send()
        swap_copy(part).wait_send()
        for way in targets:
            ref = gathered.at[part, pl.ds(0, sent[part][way]), pl.ds(0, HALF)]
            pltpu.make_async_remote_copy(
                src_ref=ref,
                dst_ref=ref,
                send_sem=gather_send.at[part, way],
                recv_sem=gather_recv.at[part, 0, 0],
                device_id=targets[way],
            ).wait_send()
    for index, (part, spots, begin, rows) in enumerate(jobs):
        par_copy(index, begin, rows).wait_send()


def shards(left_slots, right, previous, offsets, owners):
    f32 = jnp.float32
    vmem = pl.BlockSpec(memory_space=pltpu.VMEM)
    hbm = pl.BlockSpec(memory_space=pltpu.HBM)
    dma = pltpu.SemaphoreType.DMA
    operands = (offsets, owners, left_slots, right.reshape(2, KW, COLS))
    total = pl.pallas_call(
        kernel,
        out_shape=jax.ShapeDtypeStruct((KW, COLS), f32),
        in_specs=[hbm] * 4,
        out_specs=vmem,
        scratch_shapes=[
            pltpu.SMEM((ND,), jnp.int32),
            pltpu.SMEM((1, ND), jnp.int32),
            pltpu.VMEM((NROW, CH, KW), f32),
            pltpu.VMEM((NROW, CH, KW), f32),
            pltpu.VMEM((PARTS, ND, CH, KW), f32),
            pltpu.VMEM((PARTS, ND, CH, KW), f32),
            pltpu.VMEM((PARTS, NROW, ND, CH, KW), f32),
            pltpu.VMEM((NX, 2, KW, COLS), f32),
            pltpu.VMEM((ND, KW, COLS), jnp.bfloat16),
            pltpu.VMEM((ND, KW, COLS), jnp.bfloat16),
            pltpu.VMEM((KW, COLS), f32),
            pltpu.VMEM((KW, COLS), f32),
            pltpu.VMEM((KW, COLS), f32),
            dma((PARTS,)),
            dma((PARTS,)),
            dma((PARTS,)),
            dma((PARTS,)),
            dma((3, 2)),
            dma((NX, 2)),
            dma((3 + PARTS,)),
            dma((PARTS, 4)),
            dma((PARTS, NROW, 2)),
            dma((4,)),
            dma((4,)),
        ],
        compiler_params=pltpu.CompilerParams(
            collective_id=0, has_side_effects=True, vmem_limit_bytes=48 * 1024 * 1024
        ),
    )(*(pltpu.with_memory_space_constraint(a, pltpu.HBM) for a in operands))
    return 2.0 * previous - total


def solution(mesh):
    return jax.shard_map(
        shards,
        mesh=mesh,
        in_specs=(P("row", "col", None), P("col", "row"), P("col", "row"), P(), P("col", None)),
        out_specs=P("col", "row"),
        check_vma=False,
    )
```

time: 501 us -> 74 us (0.15); the launches traced: 492 us -> 73.3 us
  waiting for transfers between devices: 410 us -> 0 us
  Pallas kernels: 0 us -> 72.4 us
  loops' own time: 20.1 us -> 0 us
  between operations: 18.5 us -> 0.02 us
  matrix products: 14.3 us -> 0 us
  other arithmetic: 14.4 us -> 0.86 us
  local copies, waits for them, and re-layouts: 13.5 us -> 0.01 us
    psum x1 -> x0, waiting for transfers between devices: 243 us -> none  [spread(): return lax.psum(jnp.where(mine, array, jnp.zeros_like(array)), axis)]
    ppermute x7 -> x0, waiting for transfers between devices: 167 us -> none  [from_behind(): lax.ppermute(array, axis, [(i, (i + by) % peers) for i in range(peers)])]
    pallas_call x0 -> x1, Pallas kernels: none -> 72.4 us  [shards(): pl.pallas_call(kernel, out_shape=jax.ShapeDtypeStruct((KW, COLS), f32), i...]
    another operation x17 -> x0, loops' own time: 20.1 us -> none  [the longest x16 11.3 us: add_step(): accum = lax.cond(present, with_block, without_block, accum)]
    dot_general x6 -> x0, matrix products: 14.3 us -> none  [multiply(): jnp.dot(left_block, right_block, precision=lax.Precision.HIGHEST, preferr...]
    unnamed x16 -> x2, local copies, waits for them, and re-layouts: 10.4 us -> 0.01 us
    reduce_or x8 -> x0, other arithmetic: 5.61 us -> none  [add_step(): present = jnp.any(matched)]
  transfers between devices with their start and end apart: 8 -> 0, of which waited for: 8 -> 0; matrix products, arithmetic and copies ran while one was open for 1% -> 0% of each run, Pallas kernels for 0% -> 0%
where the time goes in v2:
time: 74 us; the launch traced here: 73.3 us
  Pallas kernels  72.4 us (98%)
  other arithmetic  0.86 us (1%)
    pallas_call x1, Pallas kernels, shards(): pl.pallas_call(kernel, out_shape=jax.ShapeDtypeStruct((KW, COLS), f32), i...  72.4 us

profile of v2, /device:TPU:6, one launch (start us, length us, event | category | flops | bytes accessed | tf_op | source)
XLA Modules:
  0.0 73.3 jit_solution(12799176708136136654)
XLA Ops:
  0.0 0.0 copy-start
  0.0 72.4 %shard_map.55 = f32[512,256]{1,0:T(8,128)S(1)} custom-call(s32[6]{0:T(128)} %offsets_hbm.1, s32[1,6]{1,0:T(1,128)} %owners_hbm.1, f32[1,512,512]{2,1,0:T(8,128)} %left.1, f32[2,512,256]{2,1,0:T(8,128)} %bitcast.1), custom_call_target="tpu_custom_call" | custom-call | tf_op jit(solution)/shard_map/pallas_call | solution.py:426
  72.4 0.0 copy-done
  72.4 0.9 %multiply_subtract_fusion = f32[512,256]{1,0:T(8,128)} fusion(f32[512,256]{1,0:T(8,128)S(1)} %shard_map.55, f32[512,256]{1,0:T(8,128)S(1)} %copy-done), kind=kLoop, calls=%fused_computation | loop fusion | flops 262144 | bytes 1572864 | tf_op jit(solution)/shard_map/sub | solution.py:461
Async XLA Ops:
  0.0 72.4 %copy-start = (f32[512,256]{1,0:T(8,128)S(1)}, f32[512,256]{1,0:T(8,128)}, u32[]{:S(2)}) copy-start(f32[512,256]{1,0:T(8,128)} %param.7) | copy-start | bytes 1572868

commit v3 on v2

--- a/solution.py
+++ b/solution.py
@@ -13,6 +13,7 @@
 COLS = 256
 PARTS = 2
 CH = KW // NROW // PARTS
+TURN = (3, 1)
 QUAD = NY * NC * CH
 SPAN = NZ * QUAD
 HALF = ND // 2
@@ -153,12 +154,13 @@
             device_id={"col": partner},
         )
 
-    def swap_copy(part):
+    def swap_copy(part, half):
+        piece = pl.ds(half * HALF, HALF)
         return pltpu.make_async_remote_copy(
-            src_ref=chosen.at[part],
-            dst_ref=partner_chosen.at[part],
-            send_sem=swap_send.at[part],
-            recv_sem=swap_recv.at[part],
+            src_ref=chosen.at[part, piece],
+            dst_ref=partner_chosen.at[part, piece],
+            send_sem=swap_send.at[part, half],
+            recv_sem=swap_recv.at[part, half],
             device_id={"col": partner},
         )
 
@@ -168,9 +170,10 @@
     def choose_stage(part):
         local_left[part].wait()
         spread_all(part).wait_recv()
-        for number in range(ND):
-            chosen[part, number] = spread[part][owners[0, number]]
-        swap_copy(part).start()
+        for half in (0, 1):
+            for number in range(half * HALF, half * HALF + HALF):
+                chosen[part, number] = spread[part][owners[0, number]]
+            swap_copy(part, half).start()
 
     beside = {"row": row_of(z, y, 1 - c)}
     across = {"row": row_of(z, 1 - y, c)}
@@ -199,16 +202,22 @@
     def receive(part, zz, yy, cc, half):
         unit_copy(part, zz, yy, cc, half, BESIDE).wait_recv()
 
-    def open_stage(part):
-        swap_copy(part).wait_recv()
-        for number in range(ND):
-            gathered[part, mine, number] = jnp.where(
-                crossing(number) == 1, partner_chosen[part, number], chosen[part, number]
-            )
-        send(part, z, y, c, 0, ACROSS, UP, DOWN)
-        send(part, z, y, c, 1, UP, DOWN, ACROSS)
-        send(part, z, y, c, 0, BESIDE)
-        send(part, z, y, c, 1, BESIDE)
+    def open_units(part):
+        def opening(half, *ways):
+            def go():
+                swap_copy(part, half).wait_recv()
+                for number in range(half * HALF, half * HALF + HALF):
+                    gathered[part, mine, number] = jnp.where(
+                        crossing(number) == 1, partner_chosen[part, number], chosen[part, number]
+                    )
+                send(part, z, y, c, half, *ways)
+
+            return go
+
+        return [
+            opening(0, ACROSS, UP, DOWN, BESIDE),
+            opening(1, UP, DOWN, ACROSS, BESIDE),
+        ]
 
     def passing(part, zz, yy, half, *ways):
         def go():
@@ -226,11 +235,12 @@
         above = (z + step) % NZ
         far = step == NZ // 2
         last = step == NZ // 2 - 1
+        early = step <= TURN[part]
         units = ((y, 0), (y, 1), (1 - y, 0))
-        if far:
+        if not early:
             units += ((1 - y, 1),)
         for yy, half in units:
-            extra = (ACROSS, BESIDE) if half == 1 and not far else (BESIDE,)
+            extra = (ACROSS, BESIDE) if half == 1 and early else (BESIDE,)
             if not (far and half == 1):
                 on = () if far or (last and half == 1) else (UP,)
                 found.append(passing(part, below, yy, half, *(on + extra)))
@@ -248,9 +258,17 @@
 
     def y_units(part, step):
         found = []
-        last = step == NZ // 2 - 1
+        if step > TURN[part]:
+            return found
         for number, zz in enumerate(places(step)):
-            on = (DOWN,) if last and number == 1 else ()
+            on = ()
+            if step == TURN[part]:
+                if step == 0:
+                    on = (UP, DOWN)
+                elif number == 1:
+                    on = (DOWN,)
+                elif step < NZ // 2 - 1:
+                    on = (UP,)
             found.append(passing(part, zz, 1 - y, 1, *(on + (BESIDE,))))
         return found
 
@@ -311,13 +329,14 @@
                 for half in (0, 1):
                     receive(part, zz, yy, 1 - c, half)
 
-    near = [spot for step in range(NZ // 2 - 1) for spot in places(step)]
-    late = [spot for step in (NZ // 2 - 1, NZ // 2) for spot in places(step)]
+    def spots_of(*steps):
+        return [spot for step in steps for spot in places(step)]
+
     jobs = []
-    for part in range(PARTS):
-        for spots in (near, late):
-            begin = jobs[-1][2] + jobs[-1][3] if jobs else 0
-            jobs.append((part, spots, begin, len(spots) * QUAD))
+    for part, steps in ((0, (0, 1, 2)), (0, (3, 4)), (1, (0, 1)), (1, (2, 3)), (1, (4,))):
+        begin = jobs[-1][2] + jobs[-1][3] if jobs else 0
+        spots = spots_of(*steps)
+        jobs.append((part, spots, begin, len(spots) * QUAD))
 
     def multiply_units(job, slices=1):
         part, spots, begin, rows = jobs[job]
@@ -334,6 +353,20 @@
             return go
 
         return [piece(index) for index in range(slices)]
+
+    def by_core(zero, one):
+        before = [dict(counts) for counts in sent]
+
+        @pl.when(c == 0)
+        def _():
+            zero()
+
+        for counts, saved in zip(sent, before):
+            counts.update(saved)
+
+        @pl.when(c == 1)
+        def _():
+            one()
 
     def run(*lists):
         longest = max(len(units) for units in lists)
@@ -370,7 +403,7 @@
         spread_stage(1, 0)
 
     spread_stage(1, 1)
-    open_stage(0)
+    run(open_units(0))
     run(neighbour_units(0))
     choose_stage(1)
     right_wait(x_west, 0)
@@ -379,23 +412,29 @@
     right_wait(x_east, 1)
     relay_west = right_copy(rights.at[x_east, 1], x_east, 1, 2, west)
     relay_west.start()
-    run(z_units(0, 1), y_units(0, 0))
+    def zero():
+        run(open_units(1))
+        run(z_units(0, 1), y_units(0, 0))
+
+    def one():
+        run(z_units(0, 1), y_units(0, 0))
+        run(open_units(1))
+
+    by_core(zero, one)
+    run(y_units(0, 1))
     run(z_units(0, 2))
-    open_stage(1)
-    run(y_units(0, 1))
-    run(z_units(0, 3), neighbour_units(1))
+    run(neighbour_units(1))
     run(y_units(0, 2))
-    run(z_units(1, 1), y_units(1, 0))
+    run(y_units(1, 0))
+    run(z_units(0, 3), z_units(1, 1))
     run(y_units(0, 3))
-    run(z_units(1, 2), z_units(0, 4))
     run(y_units(1, 1))
     prepare_right()
-    run(z_units(1, 3), multiply_units(0, 3))
-    run(y_units(1, 2))
-    run(y_units(1, 3), multiply_units(1, 3))
-    run(multiply_units(2))
-    run(z_units(1, 4))
-    run(multiply_units(3))
+    run(multiply_units(0, 3), z_units(1, 2))
+    run(z_units(0, 4), multiply_units(2, 3))
+    run(z_units(1, 3), multiply_units(1, 3))
+    run(multiply_units(3, 3), z_units(1, 4))
+    run(multiply_units(4))
     for job in range(len(jobs)):
         finish_stage(job)
 
@@ -403,7 +442,8 @@
         copy.wait_send()
     for part in range(PARTS):
         spread_all(part).wait_send()
-        swap_copy(part).wait_send()
+        for half in (0, 1):
+            swap_copy(part, half).wait_send()
         for way in targets:
             ref = gathered.at[part, pl.ds(0, sent[part][way]), pl.ds(0, HALF)]
             pltpu.make_async_remote_copy(
@@ -444,15 +484,15 @@
             pltpu.VMEM((KW, COLS), f32),
             dma((PARTS,)),
             dma((PARTS,)),
-            dma((PARTS,)),
-            dma((PARTS,)),
+            dma((PARTS, 2)),
+            dma((PARTS, 2)),
             dma((3, 2)),
             dma((NX, 2)),
             dma((3 + PARTS,)),
             dma((PARTS, 4)),
             dma((PARTS, NROW, 2)),
-            dma((4,)),
-            dma((4,)),
+            dma((5,)),
+            dma((5,)),
         ],
         compiler_params=pltpu.CompilerParams(
             collective_id=0, has_side_effects=True, vmem_limit_bytes=48 * 1024 * 1024

time: 74 us -> 71.4 us (0.965)
  Pallas kernels: 72.4 us -> 70.4 us
    pallas_call x1, Pallas kernels: 72.4 us -> 70.4 us  [shards(): pl.pallas_call(kernel, out_shape=jax.ShapeDtypeStruct((KW, COLS), f32), i...]
where the time goes in v3:
time: 71.4 us; the launch traced here: 71.3 us
  Pallas kernels  70.4 us (99%)
  other arithmetic  0.86 us (1%)
    pallas_call x1, Pallas kernels, shards(): pl.pallas_call(kernel, out_shape=jax.ShapeDtypeStruct((KW, COLS), f32), i...  70.4 us

profile of v3, /device:TPU:6, one launch (start us, length us, event | category | flops | bytes accessed | tf_op | source)
XLA Modules:
  0.0 71.3 jit_solution(10421056342125910657)
XLA Ops:
  0.0 0.0 copy-start
  0.0 70.4 %shard_map.55 = f32[512,256]{1,0:T(8,128)S(1)} custom-call(s32[6]{0:T(128)} %offsets_hbm.1, s32[1,6]{1,0:T(1,128)} %owners_hbm.1, f32[1,512,512]{2,1,0:T(8,128)} %left.1, f32[2,512,256]{2,1,0:T(8,128)} %bitcast.1), custom_call_target="tpu_custom_call" | custom-call | tf_op jit(solution)/shard_map/pallas_call | solution.py:466
  70.4 0.0 copy-done
  70.4 0.9 %multiply_subtract_fusion = f32[512,256]{1,0:T(8,128)} fusion(f32[512,256]{1,0:T(8,128)S(1)} %shard_map.55, f32[512,256]{1,0:T(8,128)S(1)} %copy-done), kind=kLoop, calls=%fused_computation | loop fusion | flops 262144 | bytes 1572864 | tf_op jit(solution)/shard_map/sub | solution.py:501
Async XLA Ops:
  0.0 70.4 %copy-start = (f32[512,256]{1,0:T(8,128)S(1)}, f32[512,256]{1,0:T(8,128)}, u32[]{:S(2)}) copy-start(f32[512,256]{1,0:T(8,128)} %param.7) | copy-start | bytes 1572868

commit v4 on v3

--- a/solution.py
+++ b/solution.py
@@ -421,14 +421,11 @@
         run(open_units(1))
 
     by_core(zero, one)
-    run(y_units(0, 1))
-    run(z_units(0, 2))
+    run(z_units(0, 2), y_units(0, 1))
     run(neighbour_units(1))
     run(y_units(0, 2))
-    run(y_units(1, 0))
-    run(z_units(0, 3), z_units(1, 1))
-    run(y_units(0, 3))
-    run(y_units(1, 1))
+    run(z_units(0, 3), z_units(1, 1), y_units(1, 0))
+    run(y_units(1, 1), y_units(0, 3))
     prepare_right()
     run(multiply_units(0, 3), z_units(1, 2))
     run(z_units(0, 4), multiply_units(2, 3))

time: 71.4 us -> 71.1 us (level)
  no operation moved by 1% of the time
where the time goes in v4:
time: 71.1 us; the launch traced here: 70.9 us
  Pallas kernels  70 us (98%)
  other arithmetic  0.86 us (1%)
    pallas_call x1, Pallas kernels, shards(): pl.pallas_call(kernel, out_shape=jax.ShapeDtypeStruct((KW, COLS), f32), i...  70 us

profile of v4, /device:TPU:6, one launch (start us, length us, event | category | flops | bytes accessed | tf_op | source)
XLA Modules:
  0.0 70.9 jit_solution(3715537825726231115)
XLA Ops:
  0.0 0.0 copy-start
  0.0 70.0 %shard_map.55 = f32[512,256]{1,0:T(8,128)S(1)} custom-call(s32[6]{0:T(128)} %offsets_hbm.1, s32[1,6]{1,0:T(1,128)} %owners_hbm.1, f32[1,512,512]{2,1,0:T(8,128)} %left.1, f32[2,512,256]{2,1,0:T(8,128)} %bitcast.1), custom_call_target="tpu_custom_call" | custom-call | tf_op jit(solution)/shard_map/pallas_call | solution.py:463
  70.1 0.0 copy-done
  70.1 0.9 %multiply_subtract_fusion = f32[512,256]{1,0:T(8,128)} fusion(f32[512,256]{1,0:T(8,128)S(1)} %shard_map.55, f32[512,256]{1,0:T(8,128)S(1)} %copy-done), kind=kLoop, calls=%fused_computation | loop fusion | flops 262144 | bytes 1572864 | tf_op jit(solution)/shard_map/sub | solution.py:498
Async XLA Ops:
  0.0 70.1 %copy-start = (f32[512,256]{1,0:T(8,128)S(1)}, f32[512,256]{1,0:T(8,128)}, u32[]{:S(2)}) copy-start(f32[512,256]{1,0:T(8,128)} %param.7) | copy-start | bytes 1572868

commit v5 on v4

--- a/solution.py
+++ b/solution.py
@@ -385,10 +385,10 @@
             place = pl.multiple_of(part * SPAN + zz * QUAD, QUAD)
             out[pl.ds(place, QUAD)] = own_sum[piece] + recv_par[piece]
 
+    for copy in first:
+        copy.start()
     spread_stage(0, 0)
     spread_stage(0, 1)
-    for copy in first:
-        copy.start()
 
     @pl.when(c == 1)
     def _():
@@ -404,14 +404,15 @@
 
     spread_stage(1, 1)
     run(open_units(0))
-    run(neighbour_units(0))
-    choose_stage(1)
     right_wait(x_west, 0)
     relay_east = right_copy(rights.at[x_west, 0], x_west, 0, 2, east)
     relay_east.start()
     right_wait(x_east, 1)
     relay_west = right_copy(rights.at[x_east, 1], x_east, 1, 2, west)
     relay_west.start()
+    run(neighbour_units(0))
+    choose_stage(1)
+
     def zero():
         run(open_units(1))
         run(z_units(0, 1), y_units(0, 0))

time: 71.1 us -> 71.2 us (level)
  no operation moved by 1% of the time
where the time goes in v5:
time: 71.2 us; the launch traced here: 70.8 us
  Pallas kernels  70 us (98%)
  other arithmetic  0.86 us (1%)
    pallas_call x1, Pallas kernels, shards(): pl.pallas_call(kernel, out_shape=jax.ShapeDtypeStruct((KW, COLS), f32), i...  70 us

profile of v5, /device:TPU:6, one launch (start us, length us, event | category | flops | bytes accessed | tf_op | source)
XLA Modules:
  0.0 70.8 jit_solution(459347857375204208)
XLA Ops:
  0.0 0.0 copy-start
  0.0 70.0 %shard_map.55 = f32[512,256]{1,0:T(8,128)S(1)} custom-call(s32[6]{0:T(128)} %offsets_hbm.1, s32[1,6]{1,0:T(1,128)} %owners_hbm.1, f32[1,512,512]{2,1,0:T(8,128)} %left.1, f32[2,512,256]{2,1,0:T(8,128)} %bitcast.1), custom_call_target="tpu_custom_call" | custom-call | tf_op jit(solution)/shard_map/pallas_call | solution.py:464
  70.0 0.0 copy-done
  70.0 0.9 %multiply_subtract_fusion = f32[512,256]{1,0:T(8,128)} fusion(f32[512,256]{1,0:T(8,128)S(1)} %shard_map.55, f32[512,256]{1,0:T(8,128)S(1)} %copy-done), kind=kLoop, calls=%fused_computation | loop fusion | flops 262144 | bytes 1572864 | tf_op jit(solution)/shard_map/sub | solution.py:499
Async XLA Ops:
  0.0 70.0 %copy-start = (f32[512,256]{1,0:T(8,128)S(1)}, f32[512,256]{1,0:T(8,128)}, u32[]{:S(2)}) copy-start(f32[512,256]{1,0:T(8,128)} %param.7) | copy-start | bytes 1572868
